TPU v7x, 32 devices: a whole 2x2x4 slice. The times are simulated.
32 devices in a mesh: dp: 4 (over z), seq: 2 (over y), tensor: 4 (over x, core).
Axes of the slice: x: 2, y: 2, z: 4, core: 2. Of those that a mesh axis runs over, the one named last changes fastest.
Arguments:
- patch_states: bfloat16 [4, 768, 4096], P('dp', 'seq', 'tensor'), may hold values from -6 to 6
- residual_grad: bfloat16 [4, 768, 4096], P('dp', 'seq', 'tensor'), may hold values from -3 to 3
- upstream_value: bfloat16 [4, 768, 512], P('dp', 'seq'), may hold values from -6 to 6
- norm_gain: bfloat16 [4096], P('tensor'), may hold values from 0.099609375 to 1.8984375
- value_weight: bfloat16 [512, 4096], P(('dp', 'seq'), 'tensor'), may hold values from -0.09375 to 0.09375
- out_weight: bfloat16 [512, 4096], P(('dp', 'seq'), 'tensor'), may hold values from -0.25 to 0.25
- attn_out: bfloat16 [4, 768, 512], P('dp', 'seq'), may hold values from -6 to 6
- queries: bfloat16 [4, 768, 512], P('dp', 'seq', 'tensor'), may hold values from -1.5 to 1.5
- byte_keys: bfloat16 [4, 16384, 512], P('dp', 'seq', 'tensor'), may hold values from -1.5 to 1.5
- byte_values: bfloat16 [4, 16384, 512], P('dp', 'seq', 'tensor'), may hold values from -6 to 6
- patch_starts: int32 [4, 768], P('dp'), may hold values from 0 to 16383, as said below
Outputs:
- wgrad_value: float32 [512, 4096], P(('dp', 'seq'), 'tensor')
- wgrad_out: float32 [512, 4096], P(('dp', 'seq'), 'tensor')
- grad_keys: bfloat16 [4, 16384, 512], P('dp', 'seq', 'tensor')
- grad_values: bfloat16 [4, 16384, 512], P('dp', 'seq', 'tensor')
Inputs may be any that keep to these rules, and one draw needn't show every extreme that they name: `patch_starts`: row i lists, increasing, the first byte of each of the 768 patches of sequence i. Every multiple of 8192 is among them, so no patch crosses the boundary between two byte shards. In every sequence one byte shard holds 768 patches, or 767 where that is fewer, and no byte shard holds more. The bytes of patch j lie on byte shard j // 384 - 1, j // 384 or j // 384 + 1.
All inputs are finite; a program needn't handle non-finite values.
Results may differ from a plain program's by a relative error of at most 0.0058.
Values may be sent and summed in bfloat16 or wider, within the bound.
A program may use at most 128 MiB of HBM per device.

v0:
```python
import functools
import math

import jax
import jax.numpy as jnp
from jax import lax
from jax.experimental import pallas as pl
from jax.experimental.pallas import tpu as pltpu
from jax.sharding import PartitionSpec as P

HD = 128


def member_sum(member32, terms):
    return lax.dot_general(
        member32,
        terms,
        (((0,), (0,)), ((), ())),
        precision=lax.Precision.HIGHEST,
        preferred_element_type=jnp.float32,
    )


def member_spread(member32, totals):
    return jnp.dot(
        member32, totals, precision=lax.Precision.HIGHEST, preferred_element_type=jnp.float32
    )


def cross_backward(member, segment_rows, keys, values, head_width):
    nbytes = keys.shape[0]
    heads = keys.shape[1] // HD
    scale = 1.0 / math.sqrt(HD)
    member32 = member.astype(jnp.float32)
    picked = jnp.dot(member, segment_rows, preferred_element_type=jnp.float32).astype(jnp.bfloat16)
    grad_f = picked[:, :head_width].astype(jnp.float32).reshape(nbytes, heads, HD)
    query_f = picked[:, head_width:].astype(jnp.float32).reshape(nbytes, heads, HD)
    keys_f = keys.astype(jnp.float32).reshape(nbytes, heads, HD)
    values_f = values.astype(jnp.float32).reshape(nbytes, heads, HD)
    scores = jnp.sum(query_f * keys_f, axis=-1) * scale
    expo = jnp.exp(scores)
    totals = member_spread(member32, member_sum(member32, expo))
    probs = expo / totals
    grad_values = (probs[..., None] * grad_f).reshape(nbytes, heads * HD).astype(jnp.bfloat16)
    prob_grad = jnp.sum(grad_f * values_f, axis=-1)
    mass = member_spread(member32, member_sum(member32, probs * prob_grad))
    score_grad = probs * (prob_grad - mass)
    grad_keys = (
        (score_grad[..., None] * query_f * scale).reshape(nbytes, heads * HD).astype(jnp.bfloat16)
    )
    return (grad_keys, grad_values)


def contract_rows(left, right):
    return lax.dot_general(
        left, right, (((0,), (0,)), ((), ())), preferred_element_type=jnp.float32
    )


def on_device(
    patch_states,
    residual_grad,
    upstream_value,
    norm_gain,
    value_weight,
    out_weight,
    attn_out,
    queries,
    byte_keys,
    byte_values,
    patch_starts,
):
    states = patch_states[0]
    patches = states.shape[0]
    width_local = states.shape[1]
    model_width = width_local * lax.axis_size("tensor")
    states32 = states.astype(jnp.float32)
    gain32 = norm_gain.astype(jnp.float32)
    upstream = upstream_value[0]
    context = attn_out[0]
    value_full, out_full = (
        lax.all_gather(value_weight, ("dp", "seq"), axis=0, tiled=True),
        lax.all_gather(out_weight, ("dp", "seq"), axis=0, tiled=True),
    )
    grad_normed = jnp.dot(upstream, value_full, preferred_element_type=jnp.float32)
    square_part = jnp.sum(states32 * states32, axis=1)
    cross_part = jnp.sum(grad_normed * gain32 * states32, axis=1)
    square_sum, cross_sum = lax.psum((square_part, cross_part), "tensor")
    inv_rms = lax.rsqrt(square_sum / model_width + 1e-05)
    normed = (states32 * inv_rms[:, None] * gain32).astype(jnp.bfloat16)
    grad_patch = (
        residual_grad[0].astype(jnp.float32)
        + inv_rms[:, None] * gain32 * grad_normed
        - (inv_rms**3)[:, None] * states32 * (cross_sum / model_width)[:, None]
    ).astype(jnp.bfloat16)
    partial_attn = lax.dot_general(
        grad_patch, out_full, (((1,), (1,)), ((), ())), preferred_element_type=jnp.float32
    )
    columns = upstream
    wgrad_value = lax.psum_scatter(
        contract_rows(columns, normed), ("dp", "seq"), scatter_dimension=0, tiled=True
    )
    columns = context
    wgrad_out = lax.psum_scatter(
        contract_rows(columns, grad_patch), ("dp", "seq"), scatter_dimension=0, tiled=True
    )
    attn_all = lax.psum(partial_attn, "tensor").astype(jnp.bfloat16)
    head_width = queries.shape[2]
    grad_attn = lax.dynamic_slice_in_dim(
        attn_all, lax.axis_index("tensor") * head_width, head_width, 1
    )
    starts = patch_starts[0]
    total_patches = starts.shape[0]
    seq_count = lax.axis_size("seq")
    seq_pos = lax.axis_index("seq")
    byte_count = byte_keys.shape[1]
    window_len = 2 * patches
    owners = starts // byte_count
    shard_ids = jnp.arange(seq_count, dtype=jnp.int32)
    firsts = jnp.sum((owners[None, :] < shard_ids[:, None]).astype(jnp.int32), axis=1)
    my_first = jnp.sum(firsts * (shard_ids == seq_pos).astype(jnp.int32))
    payload = jnp.concatenate([grad_attn, queries[0]], axis=1)
    padded_starts = jnp.concatenate(
        [starts, jnp.full((window_len,), 2 * total_patches * byte_count + byte_count, jnp.int32)]
    )
    local_starts = lax.dynamic_slice_in_dim(padded_starts, my_first, window_len)
    positions = seq_pos * byte_count + jnp.arange(byte_count, dtype=jnp.int32)
    reached = local_starts[None, :] <= positions[:, None]
    after = jnp.concatenate([reached[:, 1:], jnp.zeros((byte_count, 1), bool)], axis=1)
    member = (reached & jnp.logical_not(after)).astype(jnp.bfloat16)
    mine = seq_pos * patches + jnp.arange(patches, dtype=jnp.int32)
    targets = lax.dynamic_slice_in_dim(owners, seq_pos * patches, patches)
    target_first = jnp.sum((owners[None, :] < targets[:, None]).astype(jnp.int32), axis=1)
    slots = mine - jnp.maximum(seq_pos * patches, target_first)
    dest = targets * patches + slots
    place = (jnp.arange(seq_count * patches, dtype=jnp.int32)[:, None] == dest[None, :]).astype(
        jnp.bfloat16
    )
    outgoing = jnp.dot(place, payload, preferred_element_type=jnp.float32).astype(jnp.bfloat16)
    outgoing = outgoing.reshape(seq_count, patches, 2 * head_width)
    incoming = lax.all_to_all(outgoing, "seq", split_axis=0, concat_axis=0, tiled=True)
    wanted = my_first + jnp.arange(window_len, dtype=jnp.int32)
    sources = wanted // patches
    received_row = sources * patches + wanted - jnp.maximum(sources * patches, my_first)
    select = (
        received_row[:, None] == jnp.arange(seq_count * patches, dtype=jnp.int32)[None, :]
    ).astype(jnp.bfloat16)
    segment_rows = jnp.dot(
        select,
        incoming.reshape(seq_count * patches, 2 * head_width),
        preferred_element_type=jnp.float32,
    ).astype(jnp.bfloat16)
    grad_keys, grad_values = cross_backward(
        member, segment_rows, byte_keys[0], byte_values[0], head_width
    )
    return (wgrad_value, wgrad_out, grad_keys[None], grad_values[None])


def split3(x):
    hi = x.astype(jnp.bfloat16).astype(jnp.float32)
    rest = x - hi
    mid = rest.astype(jnp.bfloat16).astype(jnp.float32)
    return hi, mid, rest - mid


def byte_kernel(
    block, scale, bounds, rows, keys, values, gk, gv, member, picked, expo, pgrad, sums, table
):
    phase = pl.program_id(0)
    step = pl.program_id(1)
    here = pl.ds(pl.multiple_of(step * block, block), block)
    width = bounds.shape[1]
    lane = lax.broadcasted_iota(jnp.int32, (block, 128), 1)

    @pl.when((phase == 0) & (step == 0))
    def _():
        sums[...] = jnp.zeros_like(sums)

    @pl.when(phase == 0)
    def _():
        pos = step * block + lax.broadcasted_iota(jnp.int32, (block, width), 0)
        inside = (bounds[0:1, :] <= pos) & (bounds[1:2, :] > pos)
        mem = jnp.where(inside, 1.0, 0.0).astype(jnp.bfloat16)
        member[here, :] = mem
        rows_b = jnp.dot(mem, rows[...], preferred_element_type=jnp.float32)
        picked[here, :] = rows_b.astype(jnp.bfloat16)
        score = jnp.sum(rows_b[:, HD:] * keys[...].astype(jnp.float32), axis=1, keepdims=True)
        e = jnp.exp(score * scale)
        pg = jnp.sum(rows_b[:, :HD] * values[...].astype(jnp.float32), axis=1, keepdims=True)
        expo[here, :] = e
        pgrad[here, :] = pg
        cols = jnp.zeros((block, 128), jnp.float32)
        for i, part in enumerate(split3(e) + split3(e * pg)):
            cols = jnp.where(lane == i, part, cols)
        cols_t = cols.T[:16].astype(jnp.bfloat16)
        sums[...] += jnp.dot(cols_t, mem, preferred_element_type=jnp.float32)

    @pl.when((phase == 1) & (step == 0))
    def _():
        total = sums[0:1, :] + sums[1:2, :] + sums[2:3, :]
        inv = jnp.where(total > 0.0, 1.0 / jnp.where(total > 0.0, total, 1.0), 0.0)
        mass = (sums[3:4, :] + sums[4:5, :] + sums[5:6, :]) * inv
        row = lax.broadcasted_iota(jnp.int32, (128, width), 0)
        tab = jnp.zeros((128, width), jnp.float32)
        for i, part in enumerate(split3(inv) + split3(mass)):
            tab = jnp.where(row == i, part, tab)
        table[...] = tab.astype(jnp.bfloat16)

    @pl.when(phase == 1)
    def _():
        spread = lax.dot_general(
            member[here, :],
            table[...],
            (((1,), (1,)), ((), ())),
            preferred_element_type=jnp.float32,
        )
        inv = jnp.sum(jnp.where(lane < 3, spread, 0.0), axis=1, keepdims=True)
        mass = jnp.sum(jnp.where((lane >= 3) & (lane < 6), spread, 0.0), axis=1, keepdims=True)
        probs = expo[here, :] * inv
        sg = probs * (pgrad[here, :] - mass) * scale
        both = picked[here, :].astype(jnp.float32)
        gv[...] = (probs * both[:, :HD]).astype(jnp.bfloat16)
        gk[...] = (sg * both[:, HD:]).astype(jnp.bfloat16)


def byte_backward(bounds, rows, keys, values):
    nbytes = keys.shape[0]
    width = rows.shape[0]
    block = 512
    steps = nbytes // block
    shape = jax.ShapeDtypeStruct(keys.shape, jnp.bfloat16)
    return pl.pallas_call(
        functools.partial(byte_kernel, block, 1.0 / math.sqrt(HD)),
        grid=(2, steps),
        out_shape=(shape, shape),
        in_specs=[
            pl.BlockSpec((2, width), lambda p, i: (0, 0)),
            pl.BlockSpec((width, 2 * HD), lambda p, i: (0, 0)),
            pl.BlockSpec((block, HD), lambda p, i: (i * (1 - p) + (steps - 1) * p, 0)),
            pl.BlockSpec((block, HD), lambda p, i: (i * (1 - p) + (steps - 1) * p, 0)),
        ],
        out_specs=[
            pl.BlockSpec((block, HD), lambda p, i: (i * p, 0)),
            pl.BlockSpec((block, HD), lambda p, i: (i * p, 0)),
        ],
        scratch_shapes=[
            pltpu.VMEM((nbytes, width), jnp.bfloat16),
            pltpu.VMEM((nbytes, 2 * HD), jnp.bfloat16),
            pltpu.VMEM((nbytes, 1), jnp.float32),
            pltpu.VMEM((nbytes, 1), jnp.float32),
            pltpu.VMEM((16, width), jnp.float32),
            pltpu.VMEM((128, width), jnp.bfloat16),
        ],
        compiler_params=pltpu.CompilerParams(vmem_limit_bytes=56 * 1024 * 1024),
    )(bounds, rows, keys, values)


def patch_kernel(
    ndp, nt, states, resid, up, gain, vw, ow, ctx, q, wgv, wgo, pay,
    wall, sqs, sqr, part, ws, yr, zs, zr, pas, par, gn, nrm, gpat, trans, gsend, grecv, qrecv,
    s_az, r_az, s_ay, r_ay, s_sq, r_sq, s_ry, r_ry, s_rz, r_rz, s_pa, r_pa, s_g, r_g,
):
    dp, sq, tn = lax.axis_index("dp"), lax.axis_index("seq"), lax.axis_index("tensor")
    patches, width = states.shape
    model = width * nt
    mine = dp * 2 + sq
    tall = 128
    nrow = patches // tall
    ncol = width // 256

    def zdev(k):
        return (lax.rem(dp + k, ndp), sq, tn)

    def tdev(k):
        return (dp, sq, lax.rem(tn + k, nt))

    ydev = (dp, 1 - sq, tn)

    def copy(src, dst, ssem, rsem, dev):
        return pltpu.make_async_remote_copy(
            src_ref=src, dst_ref=dst, send_sem=ssem, recv_sem=rsem,
            device_id=dev, device_id_type=pl.DeviceIdType.MESH,
        )

    barrier = pltpu.get_barrier_semaphore()
    peers = [zdev(k) for k in range(1, ndp)] + [tdev(k) for k in range(1, nt)] + [ydev]
    for dev in peers:
        pl.semaphore_signal(barrier, inc=1, device_id=dev, device_id_type=pl.DeviceIdType.MESH)
    pl.semaphore_wait(barrier, len(peers))

    sent = []

    def go(c):
        c.start()
        sent.append(c)
        return c

    weights = (vw, ow)

    def gather_start(w):
        z = [
            go(copy(weights[w], wall.at[w, mine], s_az.at[w, k - 1], r_az.at[w, k - 1], zdev(k)))
            for k in range(1, ndp)
        ]
        y = [go(copy(weights[w], wall.at[w, mine], s_ay.at[w, 0], r_ay.at[w, 0], ydev))]
        return z, y

    def gather_forward(w, z, y):
        for k in range(1, ndp):
            z[k - 1].wait_recv()
            slot = lax.rem(dp + (ndp - k), ndp) * 2 + sq
            y.append(
                go(copy(wall.at[w, slot], wall.at[w, slot], s_ay.at[w, k], r_ay.at[w, k], ydev))
            )

    vz, vy = gather_start(0)
    qc = go(copy(q, qrecv, s_g.at[0], r_g.at[0], ydev))

    def row_loop(fn):
        def body(i, _):
            fn(pl.ds(pl.multiple_of(i * tall, tall), tall), i)
            return 0

        lax.fori_loop(0, nrow, body, 0)

    def to_row(col):
        return jnp.broadcast_to(col, (tall, 128)).T[:8]

    def total_of(which):
        rows = sqs[which] + sqr[which, 0]
        for k in range(1, nt - 1):
            rows = rows + sqr[which, k]
        return rows

    def share(which):
        return [
            go(copy(sqs.at[which], sqr.at[which, k - 1], s_sq.at[which, k - 1],
                    r_sq.at[which, k - 1], tdev(k)))
            for k in range(1, nt)
        ]

    def column(rows):
        return jnp.broadcast_to(rows[0:1, :], (128, patches)).T

    def square(here, i):
        x = states[here, :].astype(jnp.float32)
        sqs[0, i] = to_row(jnp.sum(x * x, axis=1, keepdims=True))

    row_loop(square)
    sq_copies = share(0)
    oz, oy = gather_start(1)
    wall[0, mine] = vw[...]
    wall[1, mine] = ow[...]
    gather_forward(0, vz, vy)
    for c in sq_copies:
        c.wait_recv()

    def inverse(i):
        rows = sqs[0, i]
        for k in range(nt - 1):
            rows = rows + sqr[0, k, i]
        col = jnp.broadcast_to(rows[0:1, :], (128, tall)).T[:, 0:1]
        return lax.rsqrt(col / model + 1e-05)

    def normalise(here, i):
        x = states[here, :].astype(jnp.float32)
        nrm[here, :] = (x * inverse(i) * gain[...].astype(jnp.float32)).astype(jnp.bfloat16)

    row_loop(normalise)

    def wgrad(w, left, right):
        trans[...] = left[...].T
        nblk, rows_per = part.shape[1], part.shape[2]

        def body(c, _):
            cols = pl.ds(pl.multiple_of(c * 256, 256), 256)
            out = jnp.dot(trans[...], right[:, cols], preferred_element_type=jnp.float32)
            part[w, :, :, cols] = out.reshape(nblk, rows_per, 256)
            return 0

        lax.fori_loop(0, ncol, body, 0)
        copies = []
        for j in range(ndp):
            ws[w, j] = part[w, j * 2 + (1 - sq)].astype(jnp.bfloat16)
            copies.append(go(copy(ws.at[w, j], yr.at[w, j], s_ry.at[w, j], r_ry.at[w, j], ydev)))
        return copies

    def wgrad_forward(w, copies):
        for c in copies:
            c.wait_recv()
        out = []
        for k in range(1, ndp):
            t = lax.rem(dp + k, ndp)
            zs[w, k - 1] = (part[w, t * 2 + sq] + yr[w, t].astype(jnp.float32)).astype(jnp.bfloat16)
            out.append(
                go(copy(zs.at[w, k - 1], zr.at[w, k - 1], s_rz.at[w, k - 1], r_rz.at[w, k - 1],
                        zdev(k)))
            )
        return out

    def wgrad_finish(w, copies, dst):
        total = part[w, mine] + yr[w, dp].astype(jnp.float32)
        for k, c in enumerate(copies):
            c.wait_recv()
            total = total + zr[w, k].astype(jnp.float32)
        dst[...] = total

    wv_y = wgrad(0, up, nrm)
    for c in vy:
        c.wait_recv()

    def project(here, i):
        full = wall[0].reshape(up.shape[1], width)
        g = jnp.dot(up[here, :], full, preferred_element_type=jnp.float32)
        gn[here, :] = g
        x = states[here, :].astype(jnp.float32)
        cross = g * gain[...].astype(jnp.float32) * x
        sqs[1, i] = to_row(jnp.sum(cross, axis=1, keepdims=True))

    row_loop(project)
    cr_copies = share(1)
    gather_forward(1, oz, oy)
    wv_z = wgrad_forward(0, wv_y)
    for c in cr_copies:
        c.wait_recv()

    def make_grad(here, i):
        inv = inverse(i)
        rows = sqs[1, i]
        for k in range(nt - 1):
            rows = rows + sqr[1, k, i]
        cross = jnp.broadcast_to(rows[0:1, :], (128, tall)).T[:, 0:1] / model
        x = states[here, :].astype(jnp.float32)
        gpat[here, :] = (
            resid[here, :].astype(jnp.float32)
            + inv * gain[...].astype(jnp.float32) * gn[here, :]
            - (inv * inv * inv * cross) * x
        ).astype(jnp.bfloat16)

    row_loop(make_grad)
    for c in oy:
        c.wait_recv()

    def attn(here, i):
        full = wall[1].reshape(up.shape[1], width)
        p = lax.dot_general(
            gpat[here, :], full, (((1,), (1,)), ((), ())), preferred_element_type=jnp.float32
        )
        for j in range(nt):
            pas[j, here, :] = p[:, j * HD : (j + 1) * HD]

    row_loop(attn)
    for k in range(1, nt):
        ws_slot = lax.rem(tn + k, nt)
        gsend[k] = pas[ws_slot].astype(jnp.bfloat16)
    pa_copies = [
        go(copy(gsend.at[k], par.at[k - 1], s_pa.at[k - 1], r_pa.at[k - 1], tdev(k)))
        for k in range(1, nt)
    ]
    wo_y = wgrad(1, ctx, gpat)
    total = pas[tn]
    for k, c in enumerate(pa_copies):
        c.wait_recv()
        total = total + par[k].astype(jnp.float32)
    gsend[0] = total.astype(jnp.bfloat16)
    gc = go(copy(gsend.at[0], grecv, s_g.at[1], r_g.at[1], ydev))
    wo_z = wgrad_forward(1, wo_y)
    wgrad_finish(0, wv_z, wgv)
    pay[sq, :, :HD] = gsend[0]
    pay[sq, :, HD:] = q[...]
    qc.wait_recv()
    gc.wait_recv()
    pay[1 - sq, :, :HD] = grecv[...]
    pay[1 - sq, :, HD:] = qrecv[...]
    wgrad_finish(1, wo_z, wgo)
    for c in sent:
        c.wait_send()


def patch_backward(ndp, nt, states, resid, up, gain, vw, ow, ctx, q):
    patches, width = states.shape
    rows = vw.shape[0]
    nblk = 2 * ndp
    bf, f32 = jnp.bfloat16, jnp.float32
    nrow = patches // 128
    vmem = pl.BlockSpec(memory_space=pltpu.VMEM)
    dma = pltpu.SemaphoreType.DMA
    return pl.pallas_call(
        functools.partial(patch_kernel, ndp, nt),
        out_shape=(
            jax.ShapeDtypeStruct((rows, width), f32),
            jax.ShapeDtypeStruct((rows, width), f32),
            jax.ShapeDtypeStruct((2, patches, 2 * HD), bf),
        ),
        in_specs=[vmem] * 8,
        out_specs=[vmem] * 3,
        scratch_shapes=[
            pltpu.VMEM((2, nblk, rows, width), bf),
            pltpu.VMEM((2, nrow, 8, 128), f32),
            pltpu.VMEM((2, nt - 1, nrow, 8, 128), f32),
            pltpu.VMEM((2, nblk, rows, width), f32),
            pltpu.VMEM((2, ndp, rows, width), bf),
            pltpu.VMEM((2, ndp, rows, width), bf),
            pltpu.VMEM((2, ndp - 1, rows, width), bf),
            pltpu.VMEM((2, ndp - 1, rows, width), bf),
            pltpu.VMEM((nt, patches, HD), f32),
            pltpu.VMEM((nt - 1, patches, HD), bf),
            pltpu.VMEM((patches, width), f32),
            pltpu.VMEM((patches, width), bf),
            pltpu.VMEM((patches, width), bf),
            pltpu.VMEM((nblk * rows, patches), bf),
            pltpu.VMEM((nt, patches, HD), bf),
            pltpu.VMEM((patches, HD), bf),
            pltpu.VMEM((patches, HD), bf),
            dma((2, ndp - 1)), dma((2, ndp - 1)),
            dma((2, ndp)), dma((2, ndp)),
            dma((2, nt - 1)), dma((2, nt - 1)),
            dma((2, ndp)), dma((2, ndp)),
            dma((2, ndp - 1)), dma((2, ndp - 1)),
            dma((nt - 1,)), dma((nt - 1,)),
            dma((2,)), dma((2,)),
        ],
        compiler_params=pltpu.CompilerParams(
            collective_id=0, has_side_effects=True, vmem_limit_bytes=56 * 1024 * 1024
        ),
    )(states, resid, up, gain, vw, ow, ctx, q)


def on_device_kernels(
    ndp, nt, patch_states, residual_grad, upstream_value, norm_gain, value_weight, out_weight,
    attn_out, queries, byte_keys, byte_values, patch_starts,
):
    wgv, wgo, pay = patch_backward(
        ndp, nt, patch_states[0], residual_grad[0], upstream_value[0], norm_gain[None],
        value_weight, out_weight, attn_out[0], queries[0],
    )
    byte_count = byte_keys.shape[1]
    starts = patch_starts[0] - lax.axis_index("seq") * byte_count
    after = jnp.concatenate([starts[1:], jnp.full((1,), 2 * byte_count, jnp.int32)])
    rows = pay.reshape(-1, 2 * HD)
    gk, gv = byte_backward(jnp.stack([starts, after]), rows, byte_keys[0], byte_values[0])
    return (wgv, wgo, gk[None], gv[None])


def solution(mesh):
    ndp, nseq, nt = mesh.shape["dp"], mesh.shape["seq"], mesh.shape["tensor"]
    use_kernels = nseq == 2 and ndp <= 4
    body = functools.partial(on_device_kernels, ndp, nt) if use_kernels else on_device
    return jax.shard_map(
        body,
        mesh=mesh,
        in_specs=(
            P("dp", "seq", "tensor"),
            P("dp", "seq", "tensor"),
            P("dp", "seq", None),
            P("tensor"),
            P(("dp", "seq"), "tensor"),
            P(("dp", "seq"), "tensor"),
            P("dp", "seq", None),
            P("dp", "seq", "tensor"),
            P("dp", "seq", "tensor"),
            P("dp", "seq", "tensor"),
            P("dp", None),
        ),
        out_specs=(
            P(("dp", "seq"), "tensor"),
            P(("dp", "seq"), "tensor"),
            P("dp", "seq", "tensor"),
            P("dp", "seq", "tensor"),
        ),
        check_vma=False,
    )
```

profile of v0, /device:TPU:28, one launch (start us, length us, event | category | flops | bytes accessed | tf_op | source)
XLA Modules:
  0.0 110.3 jit_solution(3243895125938590181)
XLA Ops:
  0.6 0.7 broadcast_subtract_fusion
  1.3 0.1 slice_reduce_fusion
  1.4 0.1 pad_add_fusion.1
  1.5 0.6 pad_add_fusion.bounds
  2.1 1.3 %broadcast_in_dim.9.gain = bf16[1,1024]{1,0:T(2,128)(2,1)} reshape(bf16[1024]{0:T(1024)(128)(2,1)} %param.14) | data formatting | bytes 4096 | tf_op jit(solution)/shard_map/broadcast_in_dim | solution.py:534
  3.4 71.3 %shard_map.138 = (f32[64,1024]{1,0:T(8,128)}, f32[64,1024]{1,0:T(8,128)}, bf16[2,384,256]{2,1,0:T(8,128)(2,1)}) custom-call(bf16[384,1024]{1,0:T(8,128)(2,1)} %bitcast.12, bf16[384,1024]{1,0:T(8,128)(2,1)} %bitcast.13, bf16[384,512]{1,0:T(8,128)(2,1)} %bitcast.15, bf16[1,1024]{1,0:T(2,128)(2,1)} %broadcast_in_dim.9.gain, bf16[64,1024]{1,0:T(8,128)(2,1)} %vw.1, ...), custom_call_target="tpu_custom_call" | custom-call | tf_op jit(solution)/shard_map/pallas_call | solution.py:488
  74.7 0.0 copy-start.1
  74.7 0.0 copy-start
  74.7 34.1 %shard_map.139 = (bf16[8192,128]{1,0:T(8,128)(2,1)}, bf16[8192,128]{1,0:T(8,128)(2,1)}) custom-call(s32[2,768]{1,0:T(2,128)} %pad_add_fusion.bounds, bf16[768,256]{1,0:T(8,128)(2,1)} %bitcast.14, bf16[8192,128]{1,0:T(8,128)(2,1)} %bitcast.10, bf16[8192,128]{1,0:T(8,128)(2,1)} %bitcast.11), custom_call_target="tpu_custom_call" | custom-call | tf_op jit(solution)/shard_map/pallas_call | solution.py:232
  108.8 0.0 copy-done.1
  108.8 0.7 copy.17
  109.5 0.0 copy-done
  109.5 0.7 copy.18
  (1 shorter events, 0.0 us)
Async XLA Ops:
  74.7 34.1 %copy-start.1 = (f32[64,1024]{1,0:T(8,128)S(1)}, f32[64,1024]{1,0:T(8,128)}, u32[]{:S(2)}) copy-start(f32[64,1024]{1,0:T(8,128)} %get-tuple-element.18) | copy-start | bytes 786436
  74.7 34.8 %copy-start = (f32[64,1024]{1,0:T(8,128)S(1)}, f32[64,1024]{1,0:T(8,128)}, u32[]{:S(2)}) copy-start(f32[64,1024]{1,0:T(8,128)} %get-tuple-element.19) | copy-start | bytes 786436
where the time goes:
time: 111 us; the launch traced here: 110 us
  Pallas kernels  105 us (95%)
  local copies, waits for them, and re-layouts  2.78 us (3%)
  other arithmetic  1.37 us (1%)
    pallas_call x1, Pallas kernels, patch_backward(): pl.pallas_call(functools.partial(patch_kernel, ndp, nt), out_shape=(jax.S...  71.3 us
    pallas_call x1, Pallas kernels, byte_backward(): pl.pallas_call(functools.partial(byte_kernel, block, 1.0 / math.sqrt(HD))...  34.1 us

commit v1 on v0

--- a/solution.py
+++ b/solution.py
@@ -163,30 +163,21 @@
     return hi, mid, rest - mid
 
 
-def byte_kernel(
-    block, scale, bounds, rows, keys, values, gk, gv, member, picked, expo, pgrad, sums, table
-):
-    phase = pl.program_id(0)
-    step = pl.program_id(1)
-    here = pl.ds(pl.multiple_of(step * block, block), block)
+def byte_sums(block, scale, first, last, bounds, rows, keys, values, member, picked, expo, pgrad, sums):
     width = bounds.shape[1]
     lane = lax.broadcasted_iota(jnp.int32, (block, 128), 1)
 
-    @pl.when((phase == 0) & (step == 0))
-    def _():
-        sums[...] = jnp.zeros_like(sums)
-
-    @pl.when(phase == 0)
-    def _():
+    def body(step, _):
+        here = pl.ds(pl.multiple_of(step * block, block), block)
         pos = step * block + lax.broadcasted_iota(jnp.int32, (block, width), 0)
         inside = (bounds[0:1, :] <= pos) & (bounds[1:2, :] > pos)
         mem = jnp.where(inside, 1.0, 0.0).astype(jnp.bfloat16)
         member[here, :] = mem
-        rows_b = jnp.dot(mem, rows[...], preferred_element_type=jnp.float32)
+        rows_b = jnp.dot(mem, rows[...].reshape(width, 2 * HD), preferred_element_type=jnp.float32)
         picked[here, :] = rows_b.astype(jnp.bfloat16)
-        score = jnp.sum(rows_b[:, HD:] * keys[...].astype(jnp.float32), axis=1, keepdims=True)
+        score = jnp.sum(rows_b[:, HD:] * keys[here, :].astype(jnp.float32), axis=1, keepdims=True)
         e = jnp.exp(score * scale)
-        pg = jnp.sum(rows_b[:, :HD] * values[...].astype(jnp.float32), axis=1, keepdims=True)
+        pg = jnp.sum(rows_b[:, :HD] * values[here, :].astype(jnp.float32), axis=1, keepdims=True)
         expo[here, :] = e
         pgrad[here, :] = pg
         cols = jnp.zeros((block, 128), jnp.float32)
@@ -194,20 +185,28 @@
             cols = jnp.where(lane == i, part, cols)
         cols_t = cols.T[:16].astype(jnp.bfloat16)
         sums[...] += jnp.dot(cols_t, mem, preferred_element_type=jnp.float32)
-
-    @pl.when((phase == 1) & (step == 0))
-    def _():
-        total = sums[0:1, :] + sums[1:2, :] + sums[2:3, :]
-        inv = jnp.where(total > 0.0, 1.0 / jnp.where(total > 0.0, total, 1.0), 0.0)
-        mass = (sums[3:4, :] + sums[4:5, :] + sums[5:6, :]) * inv
-        row = lax.broadcasted_iota(jnp.int32, (128, width), 0)
-        tab = jnp.zeros((128, width), jnp.float32)
-        for i, part in enumerate(split3(inv) + split3(mass)):
-            tab = jnp.where(row == i, part, tab)
-        table[...] = tab.astype(jnp.bfloat16)
-
-    @pl.when(phase == 1)
-    def _():
+        return 0
+
+    lax.fori_loop(first, last, body, 0)
+
+
+def byte_table(sums, table):
+    width = sums.shape[1]
+    total = sums[0:1, :] + sums[1:2, :] + sums[2:3, :]
+    inv = jnp.where(total > 0.0, 1.0 / jnp.where(total > 0.0, total, 1.0), 0.0)
+    mass = (sums[3:4, :] + sums[4:5, :] + sums[5:6, :]) * inv
+    row = lax.broadcasted_iota(jnp.int32, (128, width), 0)
+    tab = jnp.zeros((128, width), jnp.float32)
+    for i, part in enumerate(split3(inv) + split3(mass)):
+        tab = jnp.where(row == i, part, tab)
+    table[...] = tab.astype(jnp.bfloat16)
+
+
+def byte_grads(block, scale, first, last, member, picked, expo, pgrad, table, gk, gv):
+    lane = lax.broadcasted_iota(jnp.int32, (block, 128), 1)
+
+    def body(step, _):
+        here = pl.ds(pl.multiple_of(step * block, block), block)
         spread = lax.dot_general(
             member[here, :],
             table[...],
@@ -219,45 +218,18 @@
         probs = expo[here, :] * inv
         sg = probs * (pgrad[here, :] - mass) * scale
         both = picked[here, :].astype(jnp.float32)
-        gv[...] = (probs * both[:, :HD]).astype(jnp.bfloat16)
-        gk[...] = (sg * both[:, HD:]).astype(jnp.bfloat16)
-
-
-def byte_backward(bounds, rows, keys, values):
-    nbytes = keys.shape[0]
-    width = rows.shape[0]
-    block = 512
-    steps = nbytes // block
-    shape = jax.ShapeDtypeStruct(keys.shape, jnp.bfloat16)
-    return pl.pallas_call(
-        functools.partial(byte_kernel, block, 1.0 / math.sqrt(HD)),
-        grid=(2, steps),
-        out_shape=(shape, shape),
-        in_specs=[
-            pl.BlockSpec((2, width), lambda p, i: (0, 0)),
-            pl.BlockSpec((width, 2 * HD), lambda p, i: (0, 0)),
-            pl.BlockSpec((block, HD), lambda p, i: (i * (1 - p) + (steps - 1) * p, 0)),
-            pl.BlockSpec((block, HD), lambda p, i: (i * (1 - p) + (steps - 1) * p, 0)),
-        ],
-        out_specs=[
-            pl.BlockSpec((block, HD), lambda p, i: (i * p, 0)),
-            pl.BlockSpec((block, HD), lambda p, i: (i * p, 0)),
-        ],
-        scratch_shapes=[
-            pltpu.VMEM((nbytes, width), jnp.bfloat16),
-            pltpu.VMEM((nbytes, 2 * HD), jnp.bfloat16),
-            pltpu.VMEM((nbytes, 1), jnp.float32),
-            pltpu.VMEM((nbytes, 1), jnp.float32),
-            pltpu.VMEM((16, width), jnp.float32),
-            pltpu.VMEM((128, width), jnp.bfloat16),
-        ],
-        compiler_params=pltpu.CompilerParams(vmem_limit_bytes=56 * 1024 * 1024),
-    )(bounds, rows, keys, values)
+        gv[here, :] = (probs * both[:, :HD]).astype(jnp.bfloat16)
+        gk[here, :] = (sg * both[:, HD:]).astype(jnp.bfloat16)
+        return 0
+
+    lax.fori_loop(first, last, body, 0)
 
 
 def patch_kernel(
-    ndp, nt, states, resid, up, gain, vw, ow, ctx, q, wgv, wgo, pay,
+    ndp, nt, states, resid, up, gain, vw, ow, ctx, q, bounds, keys_in, values_in,
+    wgv, wgo, gk_out, gv_out,
     wall, sqs, sqr, part, ws, yr, zs, zr, pas, par, gn, nrm, gpat, trans, gsend, grecv, qrecv,
+    pay, keys, values, member, picked, expo, pgrad, sums, table, s_in, s_out,
     s_az, r_az, s_ay, r_ay, s_sq, r_sq, s_ry, r_ry, s_rz, r_rz, s_pa, r_pa, s_g, r_g,
 ):
     dp, sq, tn = lax.axis_index("dp"), lax.axis_index("seq"), lax.axis_index("tensor")
@@ -281,6 +253,11 @@
             src_ref=src, dst_ref=dst, send_sem=ssem, recv_sem=rsem,
             device_id=dev, device_id_type=pl.DeviceIdType.MESH,
         )
+
+    k_in = pltpu.make_async_copy(keys_in, keys, s_in.at[0])
+    v_in = pltpu.make_async_copy(values_in, values, s_in.at[1])
+    k_in.start()
+    v_in.start()
 
     barrier = pltpu.get_barrier_semaphore()
     peers = [zdev(k) for k in range(1, ndp)] + [tdev(k) for k in range(1, nt)] + [ydev]
@@ -405,7 +382,6 @@
             total = total + zr[w, k].astype(jnp.float32)
         dst[...] = total
 
-    wv_y = wgrad(0, up, nrm)
     for c in vy:
         c.wait_recv()
 
@@ -420,7 +396,6 @@
     row_loop(project)
     cr_copies = share(1)
     gather_forward(1, oz, oy)
-    wv_z = wgrad_forward(0, wv_y)
     for c in cr_copies:
         c.wait_recv()
 
@@ -457,30 +432,51 @@
         go(copy(gsend.at[k], par.at[k - 1], s_pa.at[k - 1], r_pa.at[k - 1], tdev(k)))
         for k in range(1, nt)
     ]
-    wo_y = wgrad(1, ctx, gpat)
+    wv_y = wgrad(0, up, nrm)
     total = pas[tn]
     for k, c in enumerate(pa_copies):
         c.wait_recv()
         total = total + par[k].astype(jnp.float32)
     gsend[0] = total.astype(jnp.bfloat16)
     gc = go(copy(gsend.at[0], grecv, s_g.at[1], r_g.at[1], ydev))
-    wo_z = wgrad_forward(1, wo_y)
-    wgrad_finish(0, wv_z, wgv)
+    wo_y = wgrad(1, ctx, gpat)
+    sums[...] = jnp.zeros_like(sums)
     pay[sq, :, :HD] = gsend[0]
     pay[sq, :, HD:] = q[...]
+    k_in.wait()
+    v_in.wait()
     qc.wait_recv()
     gc.wait_recv()
     pay[1 - sq, :, :HD] = grecv[...]
     pay[1 - sq, :, HD:] = qrecv[...]
+    block = 512
+    steps = keys.shape[0] // block
+    scale = 1.0 / math.sqrt(HD)
+    args = (bounds, pay, keys, values, member, picked, expo, pgrad, sums)
+    byte_sums(block, scale, 0, steps // 4, *args)
+    wv_z = wgrad_forward(0, wv_y)
+    byte_sums(block, scale, steps // 4, 3 * steps // 4, *args)
+    wo_z = wgrad_forward(1, wo_y)
+    byte_sums(block, scale, 3 * steps // 4, steps, *args)
+    byte_table(sums, table)
+    byte_grads(block, scale, 0, steps, member, picked, expo, pgrad, table, keys, values)
+    k_out = pltpu.make_async_copy(keys, gk_out, s_out.at[0])
+    v_out = pltpu.make_async_copy(values, gv_out, s_out.at[1])
+    k_out.start()
+    v_out.start()
+    wgrad_finish(0, wv_z, wgv)
     wgrad_finish(1, wo_z, wgo)
+    k_out.wait()
+    v_out.wait()
     for c in sent:
         c.wait_send()
 
 
-def patch_backward(ndp, nt, states, resid, up, gain, vw, ow, ctx, q):
+def patch_backward(ndp, nt, states, resid, up, gain, vw, ow, ctx, q, bounds, keys, values):
     patches, width = states.shape
     rows = vw.shape[0]
     nblk = 2 * ndp
+    nbytes = keys.shape[0]
     bf, f32 = jnp.bfloat16, jnp.float32
     nrow = patches // 128
     vmem = pl.BlockSpec(memory_space=pltpu.VMEM)
@@ -490,10 +486,11 @@
         out_shape=(
             jax.ShapeDtypeStruct((rows, width), f32),
             jax.ShapeDtypeStruct((rows, width), f32),
-            jax.ShapeDtypeStruct((2, patches, 2 * HD), bf),
+            jax.ShapeDtypeStruct(keys.shape, bf),
+            jax.ShapeDtypeStruct(keys.shape, bf),
         ),
-        in_specs=[vmem] * 8,
-        out_specs=[vmem] * 3,
+        in_specs=[vmem] * 9 + [pl.BlockSpec(memory_space=pl.ANY)] * 2,
+        out_specs=[vmem] * 2 + [pl.BlockSpec(memory_space=pl.ANY)] * 2,
         scratch_shapes=[
             pltpu.VMEM((2, nblk, rows, width), bf),
             pltpu.VMEM((2, nrow, 8, 128), f32),
@@ -512,6 +509,16 @@
             pltpu.VMEM((nt, patches, HD), bf),
             pltpu.VMEM((patches, HD), bf),
             pltpu.VMEM((patches, HD), bf),
+            pltpu.VMEM((2, patches, 2 * HD), bf),
+            pltpu.VMEM(keys.shape, bf),
+            pltpu.VMEM(keys.shape, bf),
+            pltpu.VMEM((nbytes, 2 * patches), bf),
+            pltpu.VMEM((nbytes, 2 * HD), bf),
+            pltpu.VMEM((nbytes, 1), f32),
+            pltpu.VMEM((nbytes, 1), f32),
+            pltpu.VMEM((16, 2 * patches), f32),
+            pltpu.VMEM((128, 2 * patches), bf),
+            dma((2,)), dma((2,)),
             dma((2, ndp - 1)), dma((2, ndp - 1)),
             dma((2, ndp)), dma((2, ndp)),
             dma((2, nt - 1)), dma((2, nt - 1)),
@@ -521,24 +528,23 @@
             dma((2,)), dma((2,)),
         ],
         compiler_params=pltpu.CompilerParams(
-            collective_id=0, has_side_effects=True, vmem_limit_bytes=56 * 1024 * 1024
+            collective_id=0, has_side_effects=True, vmem_limit_bytes=62 * 1024 * 1024
         ),
-    )(states, resid, up, gain, vw, ow, ctx, q)
+    )(states, resid, up, gain, vw, ow, ctx, q, bounds, keys, values)
 
 
 def on_device_kernels(
     ndp, nt, patch_states, residual_grad, upstream_value, norm_gain, value_weight, out_weight,
     attn_out, queries, byte_keys, byte_values, patch_starts,
 ):
-    wgv, wgo, pay = patch_backward(
-        ndp, nt, patch_states[0], residual_grad[0], upstream_value[0], norm_gain[None],
-        value_weight, out_weight, attn_out[0], queries[0],
-    )
     byte_count = byte_keys.shape[1]
     starts = patch_starts[0] - lax.axis_index("seq") * byte_count
     after = jnp.concatenate([starts[1:], jnp.full((1,), 2 * byte_count, jnp.int32)])
-    rows = pay.reshape(-1, 2 * HD)
-    gk, gv = byte_backward(jnp.stack([starts, after]), rows, byte_keys[0], byte_values[0])
+    wgv, wgo, gk, gv = patch_backward(
+        ndp, nt, patch_states[0], residual_grad[0], upstream_value[0], norm_gain[None],
+        value_weight, out_weight, attn_out[0], queries[0],
+        jnp.stack([starts, after]), byte_keys[0], byte_values[0],
+    )
     return (wgv, wgo, gk[None], gv[None])
 
 

time: 111 us -> 102 us (0.919)
  Pallas kernels: 105 us -> 89.4 us
  local copies, waits for them, and re-layouts: 2.78 us -> 9.23 us
    pallas_call x1 -> x0, Pallas kernels: 34.1 us -> none  [byte_backward(): pl.pallas_call(functools.partial(byte_kernel, block, 1.0 / math.sqrt(HD))...]
    pallas_call x1, Pallas kernels: 71.3 us -> 89.4 us  [patch_backward(): pl.pallas_call(functools.partial(patch_kernel, ndp, nt), out_shape=(jax.S...]
    unnamed x6, local copies, waits for them, and re-layouts: 1.41 us -> 7.86 us
where the time goes in v1:
time: 102 us; the launch traced here: 101 us
  Pallas kernels  89.4 us (88%)
  local copies, waits for them, and re-layouts  9.23 us (9%)
  other arithmetic  1.37 us (1%)
    pallas_call x1, Pallas kernels, patch_backward(): pl.pallas_call(functools.partial(patch_kernel, ndp, nt), out_shape=(jax.S...  89.4 us
    unnamed x6, local copies, waits for them, and re-layouts  7.86 us

profile of v1, /device:TPU:28, one launch (start us, length us, event | category | flops | bytes accessed | tf_op | source)
XLA Modules:
  0.0 100.7 jit_solution(17036646514320492242)
XLA Ops:
  0.6 0.7 broadcast_subtract_fusion
  1.3 0.1 slice_reduce_fusion
  1.4 0.1 pad_add_fusion.1
  1.5 0.6 pad_add_fusion.bounds
  2.1 1.3 %broadcast_in_dim.9.gain = bf16[1,1024]{1,0:T(2,128)(2,1)} reshape(bf16[1024]{0:T(1024)(128)(2,1)} %param.14) | data formatting | bytes 4096 | tf_op jit(solution)/shard_map/broadcast_in_dim | solution.py:544
  3.4 89.4 %shard_map.138 = (f32[64,1024]{1,0:T(8,128)}, f32[64,1024]{1,0:T(8,128)}, bf16[8192,128]{1,0:T(8,128)(2,1)}, bf16[8192,128]{1,0:T(8,128)(2,1)}) custom-call(bf16[384,1024]{1,0:T(8,128)(2,1)} %bitcast.13, bf16[384,1024]{1,0:T(8,128)(2,1)} %bitcast.14, bf16[384,512]{1,0:T(8,128)(2,1)} %bitcast.15, bf16[1,1024]{1,0:T(2,128)(2,1)} %broadcast_in_dim.9.gain, ...), custom_call_target="tpu_custom_call" | custom-call | tf_op jit(solution)/shard_map/pallas_call | solution.py:484
  92.8 1.7 %copy.19 = f32[64,1024]{1,0:T(8,128)} copy(f32[64,1024]{1,0:T(8,128)} %get-tuple-element.16) | data formatting | bytes 524288
  94.5 1.7 %copy.20 = f32[64,1024]{1,0:T(8,128)} copy(f32[64,1024]{1,0:T(8,128)} %get-tuple-element.17) | data formatting | bytes 524288
  96.1 0.0 copy-start
  96.1 3.2 %copy.21 = bf16[1,8192,128]{2,1,0:T(8,128)(2,1)} copy(bf16[1,8192,128]{2,1,0:T(8,128)(2,1)} %bitcast.12) | data formatting | bytes 4194304
  99.3 0.0 copy-done
  99.3 1.3 %copy.22 = bf16[1,8192,128]{2,1,0:T(8,128)(2,1)} copy(bf16[1,8192,128]{2,1,0:T(8,128)(2,1)S(1)} %bitcast.11) | data formatting | bytes 4194304
  (1 shorter events, 0.0 us)
Async XLA Ops:
  96.1 3.2 %copy-start = (bf16[8192,128]{1,0:T(8,128)(2,1)S(1)}, bf16[8192,128]{1,0:T(8,128)(2,1)}, u32[]{:S(2)}) copy-start(bf16[8192,128]{1,0:T(8,128)(2,1)} %get-tuple-element.11) | copy-start | bytes 6291460
